TPU v7x, 128 devices: a whole 4x4x4 slice. The times are simulated.
128 devices in a mesh: store: 8 (over z, core), mp: 16 (over y, x).
Axes of the slice: x: 4, y: 4, z: 4, core: 2. Of those that a mesh axis runs over, the one named last changes fastest.
Arguments:
- tokens: bfloat16 [2048, 6144], P('store', 'mp'), may hold values from -6 to 6
- gain: float32 [6144], replicated, may hold values from 0.1 to 1.9
- base_projection_weight: bfloat16 [6144, 6144], P(None, 'mp'), may hold values from -0.078125 to 0.078125
- adapter_down_weight: bfloat16 [64, 64, 6144], P('store', None, 'mp'), may hold values from -0.078125 to 0.078125
- adapter_up_weight: bfloat16 [64, 64, 6144], P('store', None, 'mp'), may hold values from -0.75 to 0.75
- plan: int32 [8, 4], replicated, may hold values from 0 to 63, as said below
- target: int32 [2048, 1], P('store'), may hold values from 0 to 7; in each aligned block of 256 rows (0 to 255, 256 to 511, ...) at most 64 rows name the same one
- slot: int32 [2048], P('store'), may hold values from 0 to 11
Outputs:
- hidden_out: bfloat16 [2048, 6144], P('store', 'mp')
Inputs may be any that keep to these rules, and one draw needn't show every extreme that they name: plan[g, r] is an adapter owned by a store group other than g; adapter a is owned by group a // 8. `target`: among the 256 rows of one store group at most 64 name the same group, a bound that some block reaches.
All inputs are finite; a program needn't handle non-finite values.
Results may differ from a plain program's by a relative error of at most 0.0063.
Values may be sent and summed in bfloat16 or wider, within the bound.
A program may use at most 64 MiB of HBM per device.

v0:
```python
import jax
import jax.numpy as jnp
from jax import lax
from jax.sharding import PartitionSpec as P

STEPS = 4
CAP = 64
adapter_scale = 0.5


def local(
    tokens, gain, base_projection_weight, adapter_down_weight, adapter_up_weight, plan, target, slot
):
    store_count = lax.axis_size("store")
    group = lax.axis_index("store")
    owned_adapters = adapter_down_weight.shape[0]
    rank_position = adapter_down_weight.shape[1]
    width_portion = adapter_down_weight.shape[2]
    replica_count = plan.shape[1]
    n_slots = owned_adapters + replica_count
    flattened_down = adapter_down_weight.reshape(owned_adapters, rank_position * width_portion)
    flattened_up = adapter_up_weight.reshape(owned_adapters, rank_position * width_portion)
    own_plan = lax.dynamic_slice_in_dim(plan, group, 1, 0)[0]
    pieces = (
        lax.all_gather(flattened_down, "store", axis=0, tiled=True),
        lax.all_gather(flattened_up, "store", axis=0, tiled=True),
    )
    count = pieces[0].shape[0]
    select = (own_plan[:, None] == jnp.arange(count, dtype=jnp.int32)[None, :]).astype(jnp.bfloat16)
    replica_down_factor = jnp.dot(select, pieces[0], preferred_element_type=jnp.float32)
    replica_up_factor = jnp.dot(select, pieces[1], preferred_element_type=jnp.float32)
    host_down = jnp.concatenate(
        [
            adapter_down_weight,
            replica_down_factor.astype(jnp.bfloat16).reshape(
                replica_count, rank_position, width_portion
            ),
        ],
        0,
    )
    host_down = host_down.reshape(n_slots * rank_position, width_portion)
    host_up = jnp.concatenate(
        [
            adapter_up_weight,
            replica_up_factor.astype(jnp.bfloat16).reshape(
                replica_count, rank_position, width_portion
            ),
        ],
        0,
    )
    host_up = host_up.reshape(n_slots * rank_position, width_portion)
    target_group = target[:, 0]
    member = (target_group[:, None] == jnp.arange(store_count, dtype=jnp.int32)[None, :]).astype(
        jnp.int32
    )
    earlier = jnp.cumsum(member, axis=0) - member
    bucket_place = jnp.sum(earlier * member, axis=1)
    row_index = target_group * CAP + bucket_place
    slot_buffer = (
        jnp.full((store_count * CAP,), -1, jnp.int32)
        .at[row_index]
        .set(slot)
        .reshape(store_count, CAP)
    )
    state = tokens
    column_start = lax.axis_index("mp") * width_portion
    for step in range(STEPS):
        whole = lax.all_gather(state, "mp", axis=1, tiled=True)
        values = whole.astype(jnp.float32)
        mean_sq = jnp.mean(values * values, axis=1, keepdims=True)
        normed = (values * lax.rsqrt(mean_sq + 1e-05) * gain[None, :]).astype(jnp.bfloat16)
        mine = lax.dynamic_slice_in_dim(normed, column_start, width_portion, 1)
        row_buffer = (
            jnp.zeros((store_count * CAP, width_portion), jnp.bfloat16).at[row_index].set(mine)
        )
        row_buffer = row_buffer.reshape(store_count, CAP, width_portion)
        rows = lax.all_to_all(row_buffer, "store", split_axis=0, concat_axis=0, tiled=True)
        slots_in = lax.all_to_all(slot_buffer, "store", split_axis=0, concat_axis=0, tiled=True)
        senders, adapter_count = slots_in.shape
        total_rows = senders * adapter_count
        flat_rows = rows.reshape(total_rows, width_portion)
        partial_value = lax.dot_general(
            flat_rows, host_down, (((1,), (1,)), ((), ())), preferred_element_type=jnp.float32
        )
        selected_adapter = (
            slots_in.reshape(total_rows)[:, None] == jnp.arange(n_slots, dtype=jnp.int32)[None, :]
        )
        partial_value = jnp.sum(
            partial_value.reshape(total_rows, n_slots, rank_position)
            * selected_adapter[:, :, None].astype(jnp.float32),
            axis=1,
        )
        summed_share = lax.psum_scatter(
            partial_value, "mp", scatter_dimension=0, tiled=True
        ).astype(jnp.bfloat16)
        inner = lax.all_gather(summed_share, "mp", axis=0, tiled=True)
        spread_rows = (
            selected_adapter[:, :, None].astype(jnp.bfloat16) * inner[:, None, :]
        ).reshape(total_rows, n_slots * rank_position)
        outer = jnp.dot(spread_rows, host_up, preferred_element_type=jnp.float32)
        outer = (
            (adapter_scale * outer)
            .astype(jnp.bfloat16)
            .reshape(senders, adapter_count, width_portion)
        )
        returned = lax.all_to_all(outer, "store", split_axis=0, concat_axis=0, tiled=True)
        delta = returned.reshape(store_count * CAP, width_portion)[row_index]
        base = jnp.dot(normed, base_projection_weight, preferred_element_type=jnp.float32)
        state = (state.astype(jnp.float32) + base + delta.astype(jnp.float32)).astype(jnp.bfloat16)
    return state


def solution(mesh):
    return jax.shard_map(
        local,
        mesh=mesh,
        in_specs=(
            P("store", "mp"),
            P(),
            P(None, "mp"),
            P("store", None, "mp"),
            P("store", None, "mp"),
            P(),
            P("store", None),
            P("store"),
        ),
        out_specs=P("store", "mp"),
        check_vma=False,
    )
```

profile of v0, /device:TPU:1, one launch (start us, length us, event | category | flops | bytes accessed | tf_op | source)
XLA Modules:
  0.0 813.4 jit_solution(17470650637500841050)
XLA Ops:
  7.3 2.0 copy.35
  9.4 2.0 copy.37
  16.6 6.8 all-to-all-start
  23.4 1.8 constant_dynamic-update-slice_fusion
  26.2 1.9 all-to-all-done
  29.9 33.1 %all-gather.7.cloned.1.call-done = bf16[256,6144]{1,0:T(8,128)(2,1)} async-done(((bf16[256,384]{1,0:T(8,128)(2,1)}), bf16[256,6144]{1,0:T(8,128)(2,1)}) %all-gather.7.cloned.1.call-update) | async-done | bytes 3145744 | tf_op jit(solution)/shard_map/all_gather | solution.py:68
  63.0 2.7 fusion
  65.8 1.8 fusion.2
  67.7 2.3 scatter_custom_fusion.1
  69.9 6.5 all-to-all-start.1
  76.4 21.6 %all-gather.9.cloned.1.call-done = bf16[64,24576]{1,0:T(8,128)(2,1)} async-done(((bf16[8,24576]{1,0:T(8,128)(2,1)}), bf16[64,24576]{1,0:T(8,128)(2,1)}) %all-gather.9.cloned.1.call-update) | async-done | bytes 3145744 | tf_op jit(solution)/shard_map/all_gather | solution.py:25
  98.0 2.5 convolution_convert_fusion.1
  101.2 2.3 multiply_reduce_fusion.3
  103.5 1.8 copy.27
  105.3 20.9 %all-gather.11.cloned.1.call-done = bf16[64,24576]{1,0:T(8,128)(2,1)} async-done(((bf16[8,24576]{1,0:T(8,128)(2,1)}), bf16[64,24576]{1,0:T(8,128)(2,1)}) %all-gather.11.cloned.1.call-update) | async-done | bytes 3145744 | tf_op jit(solution)/shard_map/all_gather | solution.py:26
  126.2 2.5 convolution_convert_fusion
  129.4 70.7 %reduce-scatter.13.cloned.1.call-done = f32[32,64]{1,0:T(8,128)} async-done(((f32[512,64]{1,0:T(8,128)}), f32[32,64]{1,0:T(8,128)}) %reduce-scatter.13.cloned.1.call-update) | async-done | bytes 8208 | tf_op jit(solution)/shard_map/reduce_scatter | solution.py:93
  200.9 17.0 %all_gather.32 = bf16[512,64]{1,0:T(8,128)(2,1)S(1)} all-gather(bf16[32,64]{1,0:T(8,128)(2,1)S(1)} %convert_element_type.128), channel_id=1, replica_groups=mesh['store'=8,'mp'=16] {'mp'}, dimensions={0}, use_global_device_ids=true | all-gather | bytes 69632 | tf_op jit(solution)/shard_map/all_gather | solution.py:96
  217.9 2.4 fusion.16
  220.4 12.9 %all-to-all-start.2 = ((bf16[8,64,384]{2,1,0:T(8,128)(2,1)}), bf16[8,64,384]{2,1,0:T(8,128)(2,1)S(1)}, u32[]{:S(2)}, u32[]{:S(2)}) async-start(bf16[8,64,384]{2,1,0:T(8,128)(2,1)} %bitcast.115), calls=%async_computation.2 | async-start | bytes 786432 | tf_op jit(solution)/shard_map/all_to_all | solution.py:106
  233.2 7.7 all-to-all-done.2
  240.9 1.8 gather_fusion
  242.8 5.0 fusion.27
  248.0 47.6 %all-gather.13.cloned.1.call-done = bf16[256,6144]{1,0:T(8,128)(2,1)} async-done(((bf16[256,384]{1,0:T(8,128)(2,1)}), bf16[256,6144]{1,0:T(8,128)(2,1)}) %all-gather.13.cloned.1.call-update) | async-done | bytes 3145744 | tf_op jit(solution)/shard_map/all_gather | solution.py:68
  295.6 2.7 fusion.3
  301.2 14.3 %all_to_all.52 = bf16[8,64,384]{2,1,0:T(8,128)(2,1)S(1)} all-to-all(bf16[8,64,384]{2,1,0:T(8,128)(2,1)S(1)} %bitcast.110), channel_id=1, replica_groups=mesh['store'=8,'mp'=16] {'store'}, dimensions={0} | all-to-all | bytes 786432 | tf_op jit(solution)/shard_map/all_to_all | solution.py:77
  318.1 69.2 %reduce-scatter.15.cloned.1.call-done = f32[32,64]{1,0:T(8,128)} async-done(((f32[512,64]{1,0:T(8,128)}), f32[32,64]{1,0:T(8,128)}) %reduce-scatter.15.cloned.1.call-update) | async-done | bytes 8208 | tf_op jit(solution)/shard_map/reduce_scatter | solution.py:93
  388.0 17.0 %all_gather.35 = bf16[512,64]{1,0:T(8,128)(2,1)S(1)} all-gather(bf16[32,64]{1,0:T(8,128)(2,1)S(1)} %convert_element_type.136), channel_id=1, replica_groups=mesh['store'=8,'mp'=16] {'mp'}, dimensions={0}, use_global_device_ids=true | all-gather | bytes 69632 | tf_op jit(solution)/shard_map/all_gather | solution.py:96
  406.7 20.7 %all_to_all.53 = bf16[8,64,384]{2,1,0:T(8,128)(2,1)S(1)} all-to-all(bf16[8,64,384]{2,1,0:T(8,128)(2,1)S(1)} %bitcast.119), channel_id=1, replica_groups=mesh['store'=8,'mp'=16] {'store'}, dimensions={0} | all-to-all | bytes 786432 | tf_op jit(solution)/shard_map/all_to_all | solution.py:106
  427.4 1.8 gather_fusion.1
  429.3 5.0 fusion.26
  434.4 47.4 %all-gather.15.cloned.1.call-done = bf16[256,6144]{1,0:T(8,128)(2,1)} async-done(((bf16[256,384]{1,0:T(8,128)(2,1)}), bf16[256,6144]{1,0:T(8,128)(2,1)}) %all-gather.15.cloned.1.call-update) | async-done | bytes 3145744 | tf_op jit(solution)/shard_map/all_gather | solution.py:68
  481.8 2.7 fusion.6
  487.3 14.3 %all_to_all.54 = bf16[8,64,384]{2,1,0:T(8,128)(2,1)S(1)} all-to-all(bf16[8,64,384]{2,1,0:T(8,128)(2,1)S(1)} %bitcast.111), channel_id=1, replica_groups=mesh['store'=8,'mp'=16] {'store'}, dimensions={0} | all-to-all | bytes 786432 | tf_op jit(solution)/shard_map/all_to_all | solution.py:77
  501.6 1.7 multiply_reduce_fusion.1
  504.2 69.2 %reduce-scatter.17.cloned.1.call-done = f32[32,64]{1,0:T(8,128)} async-done(((f32[512,64]{1,0:T(8,128)}), f32[32,64]{1,0:T(8,128)}) %reduce-scatter.17.cloned.1.call-update) | async-done | bytes 8208 | tf_op jit(solution)/shard_map/reduce_scatter | solution.py:93
  574.1 17.0 %all_gather.37 = bf16[512,64]{1,0:T(8,128)(2,1)S(1)} all-gather(bf16[32,64]{1,0:T(8,128)(2,1)S(1)} %convert_element_type.143), channel_id=1, replica_groups=mesh['store'=8,'mp'=16] {'mp'}, dimensions={0}, use_global_device_ids=true | all-gather | bytes 69632 | tf_op jit(solution)/shard_map/all_gather | solution.py:96
  592.9 20.7 %all_to_all.55 = bf16[8,64,384]{2,1,0:T(8,128)(2,1)S(1)} all-to-all(bf16[8,64,384]{2,1,0:T(8,128)(2,1)S(1)} %bitcast.121), channel_id=1, replica_groups=mesh['store'=8,'mp'=16] {'store'}, dimensions={0} | all-to-all | bytes 786432 | tf_op jit(solution)/shard_map/all_to_all | solution.py:106
  613.6 1.8 gather_fusion.2
  615.4 5.0 fusion.25
  620.5 47.4 %all-gather.17.cloned.1.call-done = bf16[256,6144]{1,0:T(8,128)(2,1)} async-done(((bf16[256,384]{1,0:T(8,128)(2,1)}), bf16[256,6144]{1,0:T(8,128)(2,1)}) %all-gather.17.cloned.1.call-update) | async-done | bytes 3145744 | tf_op jit(solution)/shard_map/all_gather | solution.py:68
  667.9 2.7 fusion.9
  673.5 14.3 %all_to_all.56 = bf16[8,64,384]{2,1,0:T(8,128)(2,1)S(1)} all-to-all(bf16[8,64,384]{2,1,0:T(8,128)(2,1)S(1)} %bitcast.109), channel_id=1, replica_groups=mesh['store'=8,'mp'=16] {'store'}, dimensions={0} | all-to-all | bytes 786432 | tf_op jit(solution)/shard_map/all_to_all | solution.py:77
  690.3 69.2 %reduce-scatter.19.cloned.1.call-done = f32[32,64]{1,0:T(8,128)} async-done(((f32[512,64]{1,0:T(8,128)}), f32[32,64]{1,0:T(8,128)}) %reduce-scatter.19.cloned.1.call-update) | async-done | bytes 8208 | tf_op jit(solution)/shard_map/reduce_scatter | solution.py:93
  760.2 17.0 %all_gather.39 = bf16[512,64]{1,0:T(8,128)(2,1)S(1)} all-gather(bf16[32,64]{1,0:T(8,128)(2,1)S(1)} %convert_element_type.150), channel_id=1, replica_groups=mesh['store'=8,'mp'=16] {'mp'}, dimensions={0}, use_global_device_ids=true | all-gather | bytes 69632 | tf_op jit(solution)/shard_map/all_gather | solution.py:96
  779.0 20.7 %all_to_all.57 = bf16[8,64,384]{2,1,0:T(8,128)(2,1)S(1)} all-to-all(bf16[8,64,384]{2,1,0:T(8,128)(2,1)S(1)} %bitcast.117), channel_id=1, replica_groups=mesh['store'=8,'mp'=16] {'store'}, dimensions={0} | all-to-all | bytes 786432 | tf_op jit(solution)/shard_map/all_to_all | solution.py:106
  799.7 1.8 gather_fusion.3
  801.5 5.0 fusion.24
  (91 shorter events, 33.4 us)
Async XLA Ops:
  6.5 19.4 %copy-start = (s32[8,4]{0,1:T(4,128)S(1)}, s32[8,4]{0,1:T(4,128)}, u32[]{:S(2)}) copy-start(s32[8,4]{0,1:T(4,128)} %param.13) | copy-start | bytes 388
  6.5 18.6 %copy-start.5 = (bf16[8,64,384]{2,1,0:T(8,128)(2,1)S(1)}, bf16[8,64,384]{2,1,0:T(8,128)(2,1)}, u32[]{:S(2)}) copy-start(bf16[8,64,384]{2,1,0:T(8,128)(2,1)} %param.12) | copy-start | bytes 1179652
  6.5 56.5 %all-gather.7.cloned.1.call-start = ((), (), s32[]{:S(2)}) async-start(), calls=%async_computation.13 | async-start | bytes 3342336 | tf_op jit(solution)/shard_map/all_gather | solution.py:68
  7.3 90.7 %all-gather.9.cloned.1.call-start = ((), (), s32[]{:S(2)}) async-start(), calls=%async_computation.14 | async-start | bytes 3538944 | tf_op jit(solution)/shard_map/all_gather | solution.py:25
  9.3 116.9 %all-gather.11.cloned.1.call-start = ((), (), s32[]{:S(2)}) async-start(), calls=%async_computation.15 | async-start | bytes 3538944 | tf_op jit(solution)/shard_map/all_gather | solution.py:26
  16.6 11.4 %all-to-all-start = ((s32[8,1,64]{2,1,0:T(1,128)}), s32[8,1,64]{2,1,0:T(1,128)S(1)}, u32[]{:S(2)}, u32[]{:S(2)}) async-start(s32[8,1,64]{2,1,0:T(1,128)} %all_to_all.33), calls=%async_computation | async-start | bytes 8192 | tf_op jit(solution)/shard_map/all_to_all | solution.py:78
  63.0 2.8 copy-start.1
  69.9 31.3 %all-to-all-start.1 = ((bf16[8,64,384]{2,1,0:T(8,128)(2,1)}), bf16[8,64,384]{2,1,0:T(8,128)(2,1)S(1)}, u32[]{:S(2)}, u32[]{:S(2)}) async-start(bf16[8,64,384]{2,1,0:T(8,128)(2,1)} %bitcast.6), calls=%async_computation.1 | async-start | bytes 786432 | tf_op jit(solution)/shard_map/all_to_all | solution.py:77
  76.4 123.8 %reduce-scatter.13.cloned.1.call-start = ((), (), s32[]{:S(2)}) async-start(), calls=%async_computation.19 | async-start | bytes 278528 | tf_op jit(solution)/shard_map/reduce_scatter | solution.py:93
  103.5 114.4 %copy-start.9 = (bf16[512,12]{0,1:T(8,128)(2,1)S(1)}, bf16[512,12]{0,1:T(8,128)(2,1)}, u32[]{:S(2)}) copy-start(bf16[512,12]{0,1:T(8,128)(2,1)} %get-tuple-element.5) | copy-start | bytes 36868
  220.4 20.6 %all-to-all-start.2 = ((bf16[8,64,384]{2,1,0:T(8,128)(2,1)}), bf16[8,64,384]{2,1,0:T(8,128)(2,1)S(1)}, u32[]{:S(2)}, u32[]{:S(2)}) async-start(bf16[8,64,384]{2,1,0:T(8,128)(2,1)} %bitcast.115), calls=%async_computation.2 | async-start | bytes 786432 | tf_op jit(solution)/shard_map/all_to_all | solution.py:106
  233.2 62.4 %all-gather.13.cloned.1.call-start = ((), (), s32[]{:S(2)}) async-start(), calls=%async_computation.16 | async-start | bytes 3342336 | tf_op jit(solution)/shard_map/all_gather | solution.py:68
  247.8 50.6 %copy-start.6 = (f32[6144]{0:T(1024)S(1)}, f32[6144]{0:T(1024)}, u32[]{:S(2)}) copy-start(f32[6144]{0:T(1024)} %param.9) | copy-start | bytes 73732
  247.8 139.4 %reduce-scatter.15.cloned.1.call-start = ((), (), s32[]{:S(2)}) async-start(), calls=%async_computation.20 | async-start | bytes 278528 | tf_op jit(solution)/shard_map/reduce_scatter | solution.py:93
  295.6 2.8 copy-start.2
  315.5 89.5 %copy-start.10 = (bf16[512,12]{0,1:T(8,128)(2,1)S(1)}, bf16[512,12]{0,1:T(8,128)(2,1)}, u32[]{:S(2)}) copy-start(bf16[512,12]{0,1:T(8,128)(2,1)} %get-tuple-element.5) | copy-start | bytes 36868
  318.0 163.8 %all-gather.15.cloned.1.call-start = ((), (), s32[]{:S(2)}) async-start(), calls=%async_computation.17 | async-start | bytes 3342336 | tf_op jit(solution)/shard_map/all_gather | solution.py:68
  434.3 50.3 %copy-start.7 = (f32[6144]{0:T(1024)S(1)}, f32[6144]{0:T(1024)}, u32[]{:S(2)}) copy-start(f32[6144]{0:T(1024)} %param.9) | copy-start | bytes 73732
  434.3 139.1 %reduce-scatter.17.cloned.1.call-start = ((), (), s32[]{:S(2)}) async-start(), calls=%async_computation.21 | async-start | bytes 278528 | tf_op jit(solution)/shard_map/reduce_scatter | solution.py:93
  481.8 2.8 copy-start.3
  501.6 89.5 %copy-start.11 = (bf16[512,12]{0,1:T(8,128)(2,1)S(1)}, bf16[512,12]{0,1:T(8,128)(2,1)}, u32[]{:S(2)}) copy-start(bf16[512,12]{0,1:T(8,128)(2,1)} %get-tuple-element.5) | copy-start | bytes 36868
  504.2 163.8 %all-gather.17.cloned.1.call-start = ((), (), s32[]{:S(2)}) async-start(), calls=%async_computation.18 | async-start | bytes 3342336 | tf_op jit(solution)/shard_map/all_gather | solution.py:68
  620.4 50.3 %copy-start.8 = (f32[6144]{0:T(1024)S(1)}, f32[6144]{0:T(1024)}, u32[]{:S(2)}) copy-start(f32[6144]{0:T(1024)} %param.9) | copy-start | bytes 73732
  620.4 139.1 %reduce-scatter.19.cloned.1.call-start = ((), (), s32[]{:S(2)}) async-start(), calls=%async_computation.22 | async-start | bytes 278528 | tf_op jit(solution)/shard_map/reduce_scatter | solution.py:93
  667.9 2.8 copy-start.4
  687.8 89.5 %copy-start.12 = (bf16[512,12]{0,1:T(8,128)(2,1)S(1)}, bf16[512,12]{0,1:T(8,128)(2,1)}, u32[]{:S(2)}) copy-start(bf16[512,12]{0,1:T(8,128)(2,1)} %get-tuple-element.5) | copy-start | bytes 36868
Sparse Core Ops, SparseCore 0:
  9.4 53.5 all-gather.6
  64.7 33.2 all-gather.8
  99.7 26.5 all-gather.10
  129.3 70.8 reduce-scatter.12
  247.9 47.6 all-gather.12
  318.1 69.0 reduce-scatter.14
  434.4 47.3 all-gather.14
  504.3 69.0 reduce-scatter.16
  620.6 47.3 all-gather.16
  690.4 69.0 reduce-scatter.18
where the time goes:
time: 815 us; the launch traced here: 813 us
  waiting for transfers between devices  507 us (62%)
  blocking collectives  173 us (21%)
  matrix products  39.8 us (5%)
  local copies, waits for them, and re-layouts  30.5 us (4%)
  starting transfers between devices  26.6 us (3%)
  other arithmetic  23 us (3%)
  between operations  13.8 us (2%)
    reduce_scatter x4, waiting for transfers between devices, local(): lax.psum_scatter(partial_value, 'mp', scatter_dimension=0, tiled=True)  278 us
    all_gather x4, waiting for transfers between devices, local(): whole = lax.all_gather(state, 'mp', axis=1, tiled=True)  176 us
    all_gather x4, blocking collectives, local(): inner = lax.all_gather(summed_share, 'mp', axis=0, tiled=True)  67.8 us
    all_to_all x3, blocking collectives, local(): lax.all_to_all(outer, 'store', split_axis=0, concat_axis=0, tiled=True)  62.2 us
    all_to_all x3, blocking collectives, local(): lax.all_to_all(row_buffer, 'store', split_axis=0, concat_axis=0, tiled=True)  42.9 us
    all_gather x1, waiting for transfers between devices, local(): lax.all_gather(flattened_down, 'store', axis=0, tiled=True)  21.6 us
    all_gather x1, waiting for transfers between devices, local(): lax.all_gather(flattened_up, 'store', axis=0, tiled=True)  20.9 us
    dot_general x4, matrix products, local(): jnp.dot(normed, base_projection_weight, preferred_element_type=jnp.float32)  20.1 us
  transfers between devices with their start and end apart: 13, of which 12 were waited for; matrix products, arithmetic and copies ran while one was open for 4% of the time, Pallas kernels for 0%

commit v1 on v0

--- a/solution.py
+++ b/solution.py
@@ -65,7 +65,13 @@
     state = tokens
     column_start = lax.axis_index("mp") * width_portion
     for step in range(STEPS):
-        whole = lax.all_gather(state, "mp", axis=1, tiled=True)
+        many = lax.axis_size("mp")
+        heap = []
+        for c in tuple(range(state.ndim)):
+            heap.append(many if c == 1 else 1)
+        whole = lax.all_to_all(
+            jnp.tile(state, heap), concat_axis=1, tiled=True, split_axis=1, axis_name="mp"
+        )
         values = whole.astype(jnp.float32)
         mean_sq = jnp.mean(values * values, axis=1, keepdims=True)
         normed = (values * lax.rsqrt(mean_sq + 1e-05) * gain[None, :]).astype(jnp.bfloat16)

time: 815 us -> 772 us (0.947)
  waiting for transfers between devices: 507 us -> 324 us
  blocking collectives: 173 us -> 306 us
  local copies, waits for them, and re-layouts: 30.5 us -> 51.2 us
  other arithmetic: 23 us -> 13.7 us
    all_gather x4 -> x0, waiting for transfers between devices: 176 us -> none  [local(): whole = lax.all_gather(state, 'mp', axis=1, tiled=True)]
    all_to_all x0 -> x4, blocking collectives: none -> 139 us  [the longest x3 127 us: local(): lax.all_to_all(jnp.tile(state, heap), concat_axis=1, tiled=True, split_ax...]
    all_to_all x1, waiting for transfers between devices: 1.86 us -> 42.7 us  [local(): lax.all_to_all(jnp.tile(state, heap), concat_axis=1, tiled=True, split_ax...]
    all_gather x1, waiting for transfers between devices: 21.6 us -> 0.01 us  [local(): lax.all_gather(flattened_down, 'store', axis=0, tiled=True)]
    all_gather x1, waiting for transfers between devices: 20.9 us -> 0.02 us  [local(): lax.all_gather(flattened_up, 'store', axis=0, tiled=True)]
    all_to_all x0 -> x4, local copies, waits for them, and re-layouts: none -> 12.7 us  [local(): lax.all_to_all(jnp.tile(state, heap), concat_axis=1, tiled=True, split_ax...]
    reduce_scatter x4, waiting for transfers between devices: 278 us -> 268 us  [local(): lax.psum_scatter(partial_value, 'mp', scatter_dimension=0, tiled=True)]
  transfers between devices with their start and end apart: 13 -> 9, of which waited for: 12 -> 7; matrix products, arithmetic and copies ran while one was open for 4% -> 3% of each run, Pallas kernels for 0% -> 0%
where the time goes in v1:
time: 772 us; the launch traced here: 770 us
  waiting for transfers between devices  324 us (42%)
  blocking collectives  306 us (40%)
  local copies, waits for them, and re-layouts  51.2 us (7%)
  matrix products  36.5 us (5%)
  starting transfers between devices  25.1 us (3%)
  between operations  14 us (2%)
  other arithmetic  13.7 us (2%)
    reduce_scatter x4, waiting for transfers between devices, local(): lax.psum_scatter(partial_value, 'mp', scatter_dimension=0, tiled=True)  268 us
    all_to_all x3, blocking collectives, local(): lax.all_to_all(jnp.tile(state, heap), concat_axis=1, tiled=True, split_ax...  127 us
    all_gather x4, blocking collectives, local(): inner = lax.all_gather(summed_share, 'mp', axis=0, tiled=True)  68 us
    all_to_all x3, blocking collectives, local(): lax.all_to_all(outer, 'store', split_axis=0, concat_axis=0, tiled=True)  62.2 us
    all_to_all x1, waiting for transfers between devices, local(): lax.all_to_all(jnp.tile(state, heap), concat_axis=1, tiled=True, split_ax...  42.7 us
    all_to_all x3, blocking collectives, local(): lax.all_to_all(row_buffer, 'store', split_axis=0, concat_axis=0, tiled=True)  37.5 us
    dot_general x4, matrix products, local(): jnp.dot(normed, base_projection_weight, preferred_element_type=jnp.float32)  17.9 us
    unnamed x66, local copies, waits for them, and re-layouts  15.6 us
  transfers between devices with their start and end apart: 9, of which 7 were waited for; matrix products, arithmetic and copies ran while one was open for 3% of the time, Pallas kernels for 0%

profile of v1, /device:TPU:1, one launch (start us, length us, event | category | flops | bytes accessed | tf_op | source)
XLA Modules:
  0.0 770.5 jit_solution(13063073132219681290)
XLA Ops:
  6.5 2.0 copy.71
  13.2 11.2 %all_to_all.76 = s32[8,1,64]{2,1,0:T(1,128)S(1)} all-to-all(s32[8,1,64]{2,1,0:T(1,128)S(1)} %all_to_all.50), channel_id=1, replica_groups=mesh['store'=8,'mp'=16] {'store'}, dimensions={0} | all-to-all | bytes 4096 | tf_op jit(solution)/shard_map/all_to_all | solution.py:84
  24.3 3.0 tile.8
  27.3 6.9 all-to-all-start
  38.4 42.7 %all-to-all-done = bf16[256,16,384]{2,0,1:T(8,128)(2,1)} async-done(((bf16[256,16,384]{2,0,1:T(8,128)(2,1)}), bf16[256,16,384]{2,0,1:T(8,128)(2,1)}, u32[]{:S(2)}, u32[]{:S(2)}) %all-to-all-start) | async-done | bytes 3145760 | tf_op jit(solution)/shard_map/all_to_all | solution.py:72
  81.1 3.2 copy.47
  86.2 1.7 copy-done.2
  88.0 2.2 scatter_custom_fusion.1
  90.3 5.1 all-to-all-start.2
  95.4 2.5 convolution_convert_fusion.1
  97.9 5.2 all-to-all-done.2
  104.7 2.5 convolution_convert_fusion
  107.8 65.7 %reduce-scatter.13.cloned.1.call-done = f32[32,64]{1,0:T(8,128)} async-done(((f32[512,64]{1,0:T(8,128)}), f32[32,64]{1,0:T(8,128)}) %reduce-scatter.13.cloned.1.call-update) | async-done | bytes 8208 | tf_op jit(solution)/shard_map/reduce_scatter | solution.py:99
  174.3 17.0 %all_gather.19 = bf16[512,64]{1,0:T(8,128)(2,1)S(1)} all-gather(bf16[32,64]{1,0:T(8,128)(2,1)S(1)} %convert_element_type.154), channel_id=1, replica_groups=mesh['store'=8,'mp'=16] {'mp'}, dimensions={0}, use_global_device_ids=true | all-gather | bytes 69632 | tf_op jit(solution)/shard_map/all_gather | solution.py:102
  191.4 2.6 fusion.12
  193.9 12.9 %all-to-all-start.3 = ((bf16[8,64,384]{2,1,0:T(8,128)(2,1)}), bf16[8,64,384]{2,1,0:T(8,128)(2,1)S(1)}, u32[]{:S(2)}, u32[]{:S(2)}) async-start(bf16[8,64,384]{2,1,0:T(8,128)(2,1)} %bitcast.139), calls=%async_computation.3 | async-start | bytes 786432 | tf_op jit(solution)/shard_map/all_to_all | solution.py:112
  206.8 7.7 all-to-all-done.3
  214.5 1.8 gather_fusion
  216.3 4.3 fusion.23
  221.4 42.2 %all_to_all.77 = bf16[256,16,384]{2,0,1:T(8,128)(2,1)} all-to-all(bf16[256,16,384]{2,0,1:T(8,128)(2,1)S(1)} %tile.9), channel_id=1, replica_groups=mesh['store'=8,'mp'=16] {'mp'}, dimensions={1} | all-to-all | bytes 6291456 | tf_op jit(solution)/shard_map/all_to_all | solution.py:72
  263.6 3.2 copy.51
  272.1 12.7 %all_to_all.78 = bf16[8,64,384]{2,1,0:T(8,128)(2,1)S(1)} all-to-all(bf16[8,64,384]{2,1,0:T(8,128)(2,1)S(1)} %bitcast.134), channel_id=1, replica_groups=mesh['store'=8,'mp'=16] {'store'}, dimensions={0} | all-to-all | bytes 786432 | tf_op jit(solution)/shard_map/all_to_all | solution.py:83
  284.8 1.7 multiply_reduce_fusion.6
  287.4 67.4 %reduce-scatter.15.cloned.1.call-done = f32[32,64]{1,0:T(8,128)} async-done(((f32[512,64]{1,0:T(8,128)}), f32[32,64]{1,0:T(8,128)}) %reduce-scatter.15.cloned.1.call-update) | async-done | bytes 8208 | tf_op jit(solution)/shard_map/reduce_scatter | solution.py:99
  355.6 16.9 %all_gather.21 = bf16[512,64]{1,0:T(8,128)(2,1)S(1)} all-gather(bf16[32,64]{1,0:T(8,128)(2,1)S(1)} %convert_element_type.164), channel_id=1, replica_groups=mesh['store'=8,'mp'=16] {'mp'}, dimensions={0}, use_global_device_ids=true | all-gather | bytes 69632 | tf_op jit(solution)/shard_map/all_gather | solution.py:102
  372.6 1.8 fusion.13
  374.5 20.7 %all_to_all.79 = bf16[8,64,384]{2,1,0:T(8,128)(2,1)S(1)} all-to-all(bf16[8,64,384]{2,1,0:T(8,128)(2,1)S(1)} %bitcast.143), channel_id=1, replica_groups=mesh['store'=8,'mp'=16] {'store'}, dimensions={0} | all-to-all | bytes 786432 | tf_op jit(solution)/shard_map/all_to_all | solution.py:112
  395.2 1.8 gather_fusion.1
  397.0 4.3 fusion.22
  402.0 42.6 %all_to_all.80 = bf16[256,16,384]{2,0,1:T(8,128)(2,1)} all-to-all(bf16[256,16,384]{2,0,1:T(8,128)(2,1)S(1)} %tile.10), channel_id=1, replica_groups=mesh['store'=8,'mp'=16] {'mp'}, dimensions={1} | all-to-all | bytes 6291456 | tf_op jit(solution)/shard_map/all_to_all | solution.py:72
  444.6 3.2 copy.55
  453.1 12.4 %all_to_all.81 = bf16[8,64,384]{2,1,0:T(8,128)(2,1)S(1)} all-to-all(bf16[8,64,384]{2,1,0:T(8,128)(2,1)S(1)} %bitcast.135), channel_id=1, replica_groups=mesh['store'=8,'mp'=16] {'store'}, dimensions={0} | all-to-all | bytes 786432 | tf_op jit(solution)/shard_map/all_to_all | solution.py:83
  465.5 1.7 multiply_reduce_fusion.5
  468.1 67.4 %reduce-scatter.17.cloned.1.call-done = f32[32,64]{1,0:T(8,128)} async-done(((f32[512,64]{1,0:T(8,128)}), f32[32,64]{1,0:T(8,128)}) %reduce-scatter.17.cloned.1.call-update) | async-done | bytes 8208 | tf_op jit(solution)/shard_map/reduce_scatter | solution.py:99
  536.3 17.2 %all_gather.22 = bf16[512,64]{1,0:T(8,128)(2,1)S(1)} all-gather(bf16[32,64]{1,0:T(8,128)(2,1)S(1)} %convert_element_type.173), channel_id=1, replica_groups=mesh['store'=8,'mp'=16] {'mp'}, dimensions={0}, use_global_device_ids=true | all-gather | bytes 69632 | tf_op jit(solution)/shard_map/all_gather | solution.py:102
  553.5 1.8 fusion.14
  555.4 20.7 %all_to_all.82 = bf16[8,64,384]{2,1,0:T(8,128)(2,1)S(1)} all-to-all(bf16[8,64,384]{2,1,0:T(8,128)(2,1)S(1)} %bitcast.145), channel_id=1, replica_groups=mesh['store'=8,'mp'=16] {'store'}, dimensions={0} | all-to-all | bytes 786432 | tf_op jit(solution)/shard_map/all_to_all | solution.py:112
  576.1 1.8 gather_fusion.2
  577.9 4.3 fusion.21
  582.9 42.6 %all_to_all.83 = bf16[256,16,384]{2,0,1:T(8,128)(2,1)} all-to-all(bf16[256,16,384]{2,0,1:T(8,128)(2,1)S(1)} %tile.11), channel_id=1, replica_groups=mesh['store'=8,'mp'=16] {'mp'}, dimensions={1} | all-to-all | bytes 6291456 | tf_op jit(solution)/shard_map/all_to_all | solution.py:72
  625.5 3.2 copy.59
  634.0 12.4 %all_to_all.84 = bf16[8,64,384]{2,1,0:T(8,128)(2,1)S(1)} all-to-all(bf16[8,64,384]{2,1,0:T(8,128)(2,1)S(1)} %bitcast.133), channel_id=1, replica_groups=mesh['store'=8,'mp'=16] {'store'}, dimensions={0} | all-to-all | bytes 786432 | tf_op jit(solution)/shard_map/all_to_all | solution.py:83
  649.0 67.5 %reduce-scatter.19.cloned.1.call-done = f32[32,64]{1,0:T(8,128)} async-done(((f32[512,64]{1,0:T(8,128)}), f32[32,64]{1,0:T(8,128)}) %reduce-scatter.19.cloned.1.call-update) | async-done | bytes 8208 | tf_op jit(solution)/shard_map/reduce_scatter | solution.py:99
  717.2 16.9 %all_gather.23 = bf16[512,64]{1,0:T(8,128)(2,1)S(1)} all-gather(bf16[32,64]{1,0:T(8,128)(2,1)S(1)} %convert_element_type.182), channel_id=1, replica_groups=mesh['store'=8,'mp'=16] {'mp'}, dimensions={0}, use_global_device_ids=true | all-gather | bytes 69632 | tf_op jit(solution)/shard_map/all_gather | solution.py:102
  734.2 1.8 fusion.15
  736.1 20.7 %all_to_all.85 = bf16[8,64,384]{2,1,0:T(8,128)(2,1)S(1)} all-to-all(bf16[8,64,384]{2,1,0:T(8,128)(2,1)S(1)} %bitcast.141), channel_id=1, replica_groups=mesh['store'=8,'mp'=16] {'store'}, dimensions={0} | all-to-all | bytes 786432 | tf_op jit(solution)/shard_map/all_to_all | solution.py:112
  756.8 1.8 gather_fusion.3
  758.6 5.0 fusion.20
  (131 shorter events, 38.6 us)
Async XLA Ops:
  6.5 28.8 %copy-start = (s32[8,4]{0,1:T(4,128)S(1)}, s32[8,4]{0,1:T(4,128)}, u32[]{:S(2)}) copy-start(s32[8,4]{0,1:T(4,128)} %param.13) | copy-start | bytes 388
  6.5 88.9 %all-gather.3.cloned.1.call-start = ((), (), s32[]{:S(2)}) async-start(), calls=%async_computation.17 | async-start | bytes 3538944 | tf_op jit(solution)/shard_map/all_gather | solution.py:25
  27.3 7.0 copy-start.14
  27.3 8.2 %copy-start.13 = (bf16[8,64,384]{2,1,0:T(8,128)(2,1)S(1)}, bf16[8,64,384]{2,1,0:T(8,128)(2,1)}, u32[]{:S(2)}) copy-start(bf16[8,64,384]{2,1,0:T(8,128)(2,1)} %param.11) | copy-start | bytes 1179652
  27.3 53.8 %all-to-all-start = ((bf16[256,16,384]{2,0,1:T(8,128)(2,1)}), bf16[256,16,384]{2,0,1:T(8,128)(2,1)}, u32[]{:S(2)}, u32[]{:S(2)}) async-start(bf16[256,16,384]{2,0,1:T(8,128)(2,1)} %tile.8), calls=%async_computation | async-start | bytes 6291456 | tf_op jit(solution)/shard_map/all_to_all | solution.py:72
  34.3 70.4 %all-gather.5.cloned.1.call-start = ((), (), s32[]{:S(2)}) async-start(), calls=%async_computation.18 | async-start | bytes 3538944 | tf_op jit(solution)/shard_map/all_gather | solution.py:26
  38.4 64.7 %copy-start.21 = (f32[512,12]{0,1:T(8,128)}, f32[512,12]{0,1:T(8,128)S(1)}, u32[]{:S(2)}) copy-start(f32[512,12]{0,1:T(8,128)S(1)} %get-tuple-element.6) | copy-start | bytes 73732
  38.4 152.9 %copy-start.25 = (bf16[512,12]{0,1:T(8,128)(2,1)}, bf16[512,12]{0,1:T(8,128)(2,1)S(1)}, u32[]{:S(2)}) copy-start(bf16[512,12]{0,1:T(8,128)(2,1)S(1)} %get-tuple-element.5) | copy-start | bytes 36868
  84.3 0.9 copy-start.15
  86.2 1.7 copy-start.2
  87.9 10.0 %copy-start.19 = (bf16[12,64,384]{2,1,0:T(8,128)(2,1)S(1)}, bf16[12,64,384]{2,1,0:T(8,128)(2,1)}, u32[]{:S(2)}) copy-start(bf16[12,64,384]{2,1,0:T(8,128)(2,1)} %constant_dynamic-update-slice_fusion) | copy-start | bytes 1769476
  90.3 12.9 %all-to-all-start.2 = ((bf16[8,64,384]{2,1,0:T(8,128)(2,1)}), bf16[8,64,384]{2,1,0:T(8,128)(2,1)S(1)}, u32[]{:S(2)}, u32[]{:S(2)}) async-start(bf16[8,64,384]{2,1,0:T(8,128)(2,1)} %bitcast.7), calls=%async_computation.2 | async-start | bytes 786432 | tf_op jit(solution)/shard_map/all_to_all | solution.py:83
  95.4 78.2 %reduce-scatter.13.cloned.1.call-start = ((), (), s32[]{:S(2)}) async-start(), calls=%async_computation.19 | async-start | bytes 278528 | tf_op jit(solution)/shard_map/reduce_scatter | solution.py:99
  97.9 9.2 %copy-start.20 = (bf16[12,64,384]{2,1,0:T(8,128)(2,1)}, bf16[12,64,384]{2,1,0:T(8,128)(2,1)S(1)}, u32[]{:S(2)}) copy-start(bf16[12,64,384]{2,1,0:T(8,128)(2,1)S(1)} %bitcast_dynamic-update-slice_fusion.1) | copy-start | bytes 1769476
  191.4 25.0 %copy-start.3 = (bf16[256,6144]{0,1:T(8,128)(2,1)S(1)}, bf16[256,6144]{0,1:T(8,128)(2,1)}, u32[]{:S(2)}) copy-start(bf16[256,6144]{0,1:T(8,128)(2,1)} %copy-done.2) | copy-start | bytes 9437188
  193.9 20.6 %all-to-all-start.3 = ((bf16[8,64,384]{2,1,0:T(8,128)(2,1)}), bf16[8,64,384]{2,1,0:T(8,128)(2,1)S(1)}, u32[]{:S(2)}, u32[]{:S(2)}) async-start(bf16[8,64,384]{2,1,0:T(8,128)(2,1)} %bitcast.139), calls=%async_computation.3 | async-start | bytes 786432 | tf_op jit(solution)/shard_map/all_to_all | solution.py:112
  206.8 148.0 %reduce-scatter.15.cloned.1.call-start = ((), (), s32[]{:S(2)}) async-start(), calls=%async_computation.20 | async-start | bytes 278528 | tf_op jit(solution)/shard_map/reduce_scatter | solution.py:99
  220.7 0.7 copy-start.12
  266.7 0.9 copy-start.16
  267.6 17.2 %copy-start.22 = (f32[512,12]{0,1:T(8,128)S(1)}, f32[512,12]{0,1:T(8,128)}, u32[]{:S(2)}) copy-start(f32[512,12]{0,1:T(8,128)} %copy-done.21) | copy-start | bytes 73732
  268.6 1.7 copy-start.6
  270.3 102.3 %copy-start.26 = (bf16[512,12]{0,1:T(8,128)(2,1)S(1)}, bf16[512,12]{0,1:T(8,128)(2,1)}, u32[]{:S(2)}) copy-start(bf16[512,12]{0,1:T(8,128)(2,1)} %copy-done.25) | copy-start | bytes 36868
  287.4 248.1 %reduce-scatter.17.cloned.1.call-start = ((), (), s32[]{:S(2)}) async-start(), calls=%async_computation.21 | async-start | bytes 278528 | tf_op jit(solution)/shard_map/reduce_scatter | solution.py:99
  372.6 24.4 %copy-start.7 = (bf16[256,6144]{0,1:T(8,128)(2,1)S(1)}, bf16[256,6144]{0,1:T(8,128)(2,1)}, u32[]{:S(2)}) copy-start(bf16[256,6144]{0,1:T(8,128)(2,1)} %copy-done.6) | copy-start | bytes 9437188
  401.3 0.7 copy-start.11
  447.8 0.9 copy-start.17
  448.6 16.9 %copy-start.23 = (f32[512,12]{0,1:T(8,128)S(1)}, f32[512,12]{0,1:T(8,128)}, u32[]{:S(2)}) copy-start(f32[512,12]{0,1:T(8,128)} %copy-done.21) | copy-start | bytes 73732
  449.6 1.7 copy-start.8
  451.3 102.2 %copy-start.27 = (bf16[512,12]{0,1:T(8,128)(2,1)S(1)}, bf16[512,12]{0,1:T(8,128)(2,1)}, u32[]{:S(2)}) copy-start(bf16[512,12]{0,1:T(8,128)(2,1)} %copy-done.25) | copy-start | bytes 36868
  468.1 248.4 %reduce-scatter.19.cloned.1.call-start = ((), (), s32[]{:S(2)}) async-start(), calls=%async_computation.22 | async-start | bytes 278528 | tf_op jit(solution)/shard_map/reduce_scatter | solution.py:99
  553.5 24.4 %copy-start.9 = (bf16[256,6144]{0,1:T(8,128)(2,1)S(1)}, bf16[256,6144]{0,1:T(8,128)(2,1)}, u32[]{:S(2)}) copy-start(bf16[256,6144]{0,1:T(8,128)(2,1)} %copy-done.8) | copy-start | bytes 9437188
  582.2 0.7 copy-start.10
  628.7 0.9 copy-start.18
  629.5 16.9 %copy-start.24 = (f32[512,12]{0,1:T(8,128)S(1)}, f32[512,12]{0,1:T(8,128)}, u32[]{:S(2)}) copy-start(f32[512,12]{0,1:T(8,128)} %copy-done.21) | copy-start | bytes 73732
  630.6 1.7 copy-start.4
  632.2 102.0 %copy-start.28 = (bf16[512,12]{0,1:T(8,128)(2,1)S(1)}, bf16[512,12]{0,1:T(8,128)(2,1)}, u32[]{:S(2)}) copy-start(bf16[512,12]{0,1:T(8,128)(2,1)} %copy-done.25) | copy-start | bytes 36868
  734.2 24.4 %copy-start.5 = (bf16[256,6144]{0,1:T(8,128)(2,1)S(1)}, bf16[256,6144]{0,1:T(8,128)(2,1)}, u32[]{:S(2)}) copy-start(bf16[256,6144]{0,1:T(8,128)(2,1)} %copy-done.4) | copy-start | bytes 9437188
  758.6 5.0 copy-start.1
Sparse Core Ops, SparseCore 0:
  9.0 31.5 all-gather.2
  42.3 27.6 all-gather.4
  104.8 68.7 reduce-scatter.12
  287.5 67.2 reduce-scatter.14
  468.2 67.2 reduce-scatter.16
  649.1 67.2 reduce-scatter.18
